TPU v7x, 32 devices: a whole 2x2x4 slice. The times are simulated.
32 devices in a mesh: dp: 8 (over y, x, core), tensor: 4 (over z).
Axes of the slice: x: 2, y: 2, z: 4, core: 2. Of those that a mesh axis runs over, the one named last changes fastest.
Arguments:
- inputs: bfloat16 [16384, 1024], P(('dp', 'tensor')), may hold values from -6 to 6
- lengths: int32 [8], P('dp'), may hold values from 1024 to 2048, as said below
- query_weight: bfloat16 [1024, 1024], P('dp', 'tensor'), may hold values from -0.1875 to 0.1875
- key_weight: bfloat16 [1024, 1024], P('dp', 'tensor'), may hold values from -0.1875 to 0.1875
- value_weight: bfloat16 [1024, 1024], P('dp', 'tensor'), may hold values from -0.1875 to 0.1875
- query_bias: bfloat16 [16, 64], P('tensor', 'dp'), may hold values from -3 to 3
- value_bias: bfloat16 [16, 64], P('tensor', 'dp'), may hold values from -0.29882812 to 0.29882812
- output_weight: bfloat16 [1024, 1024], P('tensor', 'dp'), may hold values from -4 to 4
- output_bias: float32 [1024], P(('dp', 'tensor')), may hold values from -3 to 3
- first_gain: float32 [1024], P(('dp', 'tensor')), may hold values from 0.5 to 1.5
- first_shift: float32 [1024], P(('dp', 'tensor')), may hold values from -1 to 1
- inner_weight: bfloat16 [1024, 4096], P('dp', 'tensor'), may hold values from -0.1875 to 0.1875
- inner_bias: bfloat16 [64, 64], P('tensor', 'dp'), may hold values from -3 to 3
- outer_weight: bfloat16 [4096, 1024], P('tensor', 'dp'), may hold values from -0.09375 to 0.09375
- outer_bias: float32 [1024], P(('dp', 'tensor')), may hold values from -3 to 3
- second_gain: float32 [1024], P(('dp', 'tensor')), may hold values from 0.5 to 1.5
- second_shift: float32 [1024], P(('dp', 'tensor')), may hold values from -1 to 1
- cotangent: bfloat16 [16384, 1024], P(('dp', 'tensor')), may hold values from -6 to 6
Outputs:
- layer_output: bfloat16 [16384, 1024], P(('dp', 'tensor'))
- input_grad: float32 [16384, 1024], P(('dp', 'tensor'))
- query_weight_grad: float32 [1024, 1024], P('dp', 'tensor')
- key_weight_grad: float32 [1024, 1024], P('dp', 'tensor')
- value_weight_grad: float32 [1024, 1024], P('dp', 'tensor')
- query_bias_grad: float32 [16, 64], P('tensor', 'dp')
- value_bias_grad: float32 [16, 64], P('tensor', 'dp')
- output_weight_grad: float32 [1024, 1024], P('tensor', 'dp')
- output_bias_grad: float32 [1024], P(('dp', 'tensor'))
- first_gain_grad: float32 [1024], P(('dp', 'tensor'))
- first_shift_grad: float32 [1024], P(('dp', 'tensor'))
- inner_weight_grad: float32 [1024, 4096], P('dp', 'tensor')
- inner_bias_grad: float32 [64, 64], P('tensor', 'dp')
- outer_weight_grad: float32 [4096, 1024], P('tensor', 'dp')
- outer_bias_grad: float32 [1024], P(('dp', 'tensor'))
- second_gain_grad: float32 [1024], P(('dp', 'tensor'))
- second_shift_grad: float32 [1024], P(('dp', 'tensor'))
Inputs may be any that keep to these rules, and one draw needn't show every extreme that they name: `lengths`: each sequence's length; one sequence has exactly 2048 and one exactly 1024.
All inputs are finite; a program needn't handle non-finite values.
Results may differ from a plain program's by a relative error of at most 0.018.
Values may be sent and summed in bfloat16 or wider, within the bound.
A program may use at most 128 MiB of HBM per device.

v0:
```python
import jax
import jax.numpy as jnp
from jax import lax
from jax.sharding import PartitionSpec as P

HEAD_DIM = 64


EPSILON = 1e-12
NEG_LARGE = 1000000000.0


def contract_rows(left, right):
    return lax.dot_general(
        left, right, (((0,), (0,)), ((), ())), preferred_element_type=jnp.float32
    )


def contract_cols(left, right):
    return lax.dot_general(
        left, right, (((1,), (1,)), ((), ())), preferred_element_type=jnp.float32
    )


def plain_product(left, right):
    return jnp.dot(left, right, preferred_element_type=jnp.float32)


def gelu_exact(value):
    return jax.nn.gelu(value, approximate=False)


def norm_forward(hidden, gain, shift):
    center = hidden - jnp.mean(hidden, -1, keepdims=True)
    inverse = lax.rsqrt(jnp.mean(center * center, -1, keepdims=True) + EPSILON)
    normed = center * inverse
    return (normed * gain + shift, normed, inverse)


def norm_backward(grad_out, normed, inverse, gain):
    grad_norm = grad_out * gain
    grad_hidden = inverse * (
        grad_norm
        - jnp.mean(grad_norm, -1, keepdims=True)
        - normed * jnp.mean(grad_norm * normed, -1, keepdims=True)
    )
    return (grad_hidden, jnp.sum(grad_out * normed, 0), jnp.sum(grad_out, 0))


def gather_sequence(local_rows):
    return lax.all_gather(local_rows, "tensor", axis=0, tiled=True)


def scatter_sequence(partial_sum):
    return lax.psum_scatter(partial_sum, "tensor", scatter_dimension=0, tiled=True)


def gather_gradient(local_rows):
    return lax.all_gather(local_rows, "tensor", axis=0, tiled=True)


def scatter_gradient(partial_sum):
    return lax.psum_scatter(
        partial_sum.astype(jnp.bfloat16), "tensor", scatter_dimension=0, tiled=True
    ).astype(jnp.float32)


def fetch_attention(query_weight, key_weight, value_weight, query_bias, value_bias, output_weight):
    return (
        lax.all_gather(query_weight, "dp", axis=0, tiled=True),
        lax.all_gather(key_weight, "dp", axis=0, tiled=True),
        lax.all_gather(value_weight, "dp", axis=0, tiled=True),
        lax.all_gather(query_bias, "dp", axis=1, tiled=True),
        lax.all_gather(value_bias, "dp", axis=1, tiled=True),
        lax.all_gather(output_weight, "dp", axis=1, tiled=True),
    )


def fetch_feedforward(inner_weight, inner_bias, outer_weight):
    return (
        lax.all_gather(inner_weight, "dp", axis=0, tiled=True),
        lax.all_gather(inner_bias, "dp", axis=1, tiled=True),
        lax.all_gather(outer_weight, "dp", axis=1, tiled=True),
    )


def split_heads(matrix):
    return matrix.reshape(matrix.shape[0], matrix.shape[1] // HEAD_DIM, HEAD_DIM).transpose(1, 0, 2)


def merge_heads(stacked):
    return stacked.transpose(1, 0, 2).reshape(stacked.shape[1], stacked.shape[0] * HEAD_DIM)


def attend_forward(query_rows, key_rows, value_rows, key_bias):
    seq_len = query_rows.shape[0]
    block_rows = min(512, seq_len)
    block_count = seq_len // block_rows
    score_scale = HEAD_DIM ** (-0.5)

    def one_head(operands):
        head_query, head_key, head_value = operands

        def one_block(query_block):
            scores = contract_cols(query_block, head_key) * score_scale + key_bias
            highest = jnp.max(scores, -1, keepdims=True)
            exponent = jnp.exp(scores - highest)
            totals = jnp.sum(exponent, -1, keepdims=True)
            weights_low = (exponent / totals).astype(jnp.bfloat16)
            context = plain_product(weights_low, head_value)
            return (context, (highest + jnp.log(totals))[:, 0])

        context, logsum = lax.map(one_block, head_query.reshape(block_count, block_rows, HEAD_DIM))
        return (context.reshape(seq_len, HEAD_DIM), logsum.reshape(seq_len))

    context, logsum = lax.map(
        one_head, (split_heads(query_rows), split_heads(key_rows), split_heads(value_rows))
    )
    return (merge_heads(context), logsum)


def attend_backward(query_rows, key_rows, value_rows, key_bias, logsum, grad_context):
    seq_len = query_rows.shape[0]
    block_rows = min(512, seq_len)
    block_count = seq_len // block_rows
    score_scale = HEAD_DIM ** (-0.5)

    def one_head(operands):
        head_query, head_key, head_value, head_logsum, head_grad = operands

        def one_block(carry, pieces):
            grad_key, grad_value = carry
            query_block, logsum_block, grad_block = pieces
            scores = contract_cols(query_block, head_key) * score_scale + key_bias
            weights = jnp.exp(scores - logsum_block[:, None])
            grad_value = grad_value + contract_rows(weights.astype(jnp.bfloat16), grad_block)
            grad_weights = contract_cols(grad_block, head_value)
            centered = grad_weights - jnp.sum(weights * grad_weights, -1, keepdims=True)
            grad_scores = (weights * centered * score_scale).astype(jnp.bfloat16)
            grad_query = plain_product(grad_scores, head_key).astype(jnp.bfloat16)
            grad_key = grad_key + contract_rows(grad_scores, query_block)
            return ((grad_key, grad_value), grad_query)

        zeros_init = jnp.zeros((seq_len, HEAD_DIM), jnp.float32)
        pieces = (
            head_query.reshape(block_count, block_rows, HEAD_DIM),
            head_logsum.reshape(block_count, block_rows),
            head_grad.reshape(block_count, block_rows, HEAD_DIM),
        )
        (grad_key, grad_value), grad_query = lax.scan(one_block, (zeros_init, zeros_init), pieces)
        return (
            grad_query.reshape(seq_len, HEAD_DIM),
            grad_key.astype(jnp.bfloat16),
            grad_value.astype(jnp.bfloat16),
        )

    grad_q, grad_k, grad_v = lax.map(
        one_head,
        (
            split_heads(query_rows),
            split_heads(key_rows),
            split_heads(value_rows),
            logsum,
            split_heads(grad_context),
        ),
    )
    return (merge_heads(grad_q), merge_heads(grad_k), merge_heads(grad_v))


def body(
    inputs,
    lengths,
    query_weight,
    key_weight,
    value_weight,
    query_bias,
    value_bias,
    output_weight,
    output_bias,
    first_gain,
    first_shift,
    inner_weight,
    inner_bias,
    outer_weight,
    outer_bias,
    second_gain,
    second_shift,
    cotangent,
):
    local_rows = inputs.shape[0]
    seq_len = local_rows * lax.axis_size("tensor")
    positions = jnp.arange(seq_len, dtype=jnp.int32)
    valid_all = (positions < lengths[0]).astype(jnp.float32)
    key_bias = (valid_all - 1.0) * NEG_LARGE
    valid_mine = lax.dynamic_slice_in_dim(
        valid_all, lax.axis_index("tensor") * local_rows, local_rows
    )[:, None]
    vectors = lax.all_gather(
        jnp.stack([output_bias, first_gain, first_shift, outer_bias, second_gain, second_shift]),
        ("dp", "tensor"),
        axis=1,
        tiled=True,
    )
    bias_out, gain_one, shift_one = (vectors[0], vectors[1], vectors[2])
    bias_two, gain_two, shift_two = (vectors[3], vectors[4], vectors[5])
    attention_set = fetch_attention(
        query_weight, key_weight, value_weight, query_bias, value_bias, output_weight
    )
    full_query, full_key, full_value, bias_query, bias_value, full_output = attention_set
    seq_inputs = gather_sequence(inputs)
    query_rows = (
        plain_product(seq_inputs, full_query) + bias_query.reshape(-1).astype(jnp.float32)
    ).astype(jnp.bfloat16)
    key_rows = plain_product(seq_inputs, full_key).astype(jnp.bfloat16)
    value_rows = (
        plain_product(seq_inputs, full_value) + bias_value.reshape(-1).astype(jnp.float32)
    ).astype(jnp.bfloat16)
    context, logsum = attend_forward(query_rows, key_rows, value_rows, key_bias)
    context_low = context.astype(jnp.bfloat16)
    attention_mine = scatter_sequence(plain_product(context_low, full_output))
    hidden_one = inputs.astype(jnp.float32) + attention_mine + bias_out
    middle, normed_one, inverse_one = norm_forward(hidden_one, gain_one, shift_one)
    feed_set = fetch_feedforward(inner_weight, inner_bias, outer_weight)
    full_inner, bias_inner, full_outer = feed_set
    seq_middle = gather_sequence(middle.astype(jnp.bfloat16))
    pre_act = plain_product(seq_middle, full_inner) + bias_inner.reshape(-1).astype(jnp.float32)
    act_low = gelu_exact(pre_act).astype(jnp.bfloat16)
    mlp_mine = scatter_sequence(plain_product(act_low, full_outer))
    hidden_two = middle + mlp_mine + bias_two
    final, normed_two, inverse_two = norm_forward(hidden_two, gain_two, shift_two)
    layer_output = (final * valid_mine).astype(jnp.bfloat16)
    back_attention = fetch_attention(
        query_weight, key_weight, value_weight, query_bias, value_bias, output_weight
    )
    back_feed = fetch_feedforward(inner_weight, inner_bias, outer_weight)
    grad_final = cotangent.astype(jnp.float32) * valid_mine
    grad_two, grad_gain_two, grad_shift_two = norm_backward(
        grad_final, normed_two, inverse_two, gain_two
    )
    grad_bias_two = jnp.sum(grad_two, 0)
    seq_grad_two = gather_gradient(grad_two.astype(jnp.bfloat16))
    grad_outer = contract_rows(act_low, seq_grad_two)
    grad_act = contract_cols(seq_grad_two, back_feed[2])
    gelu_pull = jax.vjp(gelu_exact, pre_act)[1]
    grad_pre = gelu_pull(grad_act)[0].astype(jnp.bfloat16)
    grad_inner_bias = jnp.sum(grad_pre.astype(jnp.float32), 0).reshape(bias_inner.shape)
    grad_inner = contract_rows(seq_middle, grad_pre)
    grad_middle = grad_two + scatter_gradient(contract_cols(grad_pre, back_feed[0]))
    grad_one, grad_gain_one, grad_shift_one = norm_backward(
        grad_middle, normed_one, inverse_one, gain_one
    )
    grad_bias_out = jnp.sum(grad_one, 0)
    seq_grad_one = gather_gradient(grad_one.astype(jnp.bfloat16))
    grad_output_weight = contract_rows(context_low, seq_grad_one)
    grad_context = contract_cols(seq_grad_one, back_attention[5]).astype(jnp.bfloat16)
    grad_queries, grad_keys, grad_values = attend_backward(
        query_rows, key_rows, value_rows, key_bias, logsum, grad_context
    )
    grad_query_bias = jnp.sum(grad_queries.astype(jnp.float32), 0).reshape(bias_query.shape)
    grad_value_bias = jnp.sum(grad_values.astype(jnp.float32), 0).reshape(bias_value.shape)
    grad_query_weight = contract_rows(seq_inputs, grad_queries)
    grad_key_weight = contract_rows(seq_inputs, grad_keys)
    grad_value_weight = contract_rows(seq_inputs, grad_values)
    input_part = (
        contract_cols(grad_queries, back_attention[0])
        + contract_cols(grad_keys, back_attention[1])
        + contract_cols(grad_values, back_attention[2])
    )
    input_grad = grad_one + scatter_gradient(input_part)
    owned_all = (
        lax.psum_scatter(grad_query_weight, "dp", scatter_dimension=0, tiled=True),
        lax.psum_scatter(grad_key_weight, "dp", scatter_dimension=0, tiled=True),
        lax.psum_scatter(grad_value_weight, "dp", scatter_dimension=0, tiled=True),
        lax.psum_scatter(grad_query_bias, "dp", scatter_dimension=1, tiled=True),
        lax.psum_scatter(grad_value_bias, "dp", scatter_dimension=1, tiled=True),
        lax.psum_scatter(grad_output_weight, "dp", scatter_dimension=1, tiled=True),
        lax.psum_scatter(grad_inner, "dp", scatter_dimension=0, tiled=True),
        lax.psum_scatter(grad_inner_bias, "dp", scatter_dimension=1, tiled=True),
        lax.psum_scatter(grad_outer, "dp", scatter_dimension=1, tiled=True),
    )
    owned_attention = owned_all[:6]
    owned_feed = owned_all[6:]
    owned_vectors = lax.psum_scatter(
        jnp.stack(
            [
                grad_bias_out,
                grad_gain_one,
                grad_shift_one,
                grad_bias_two,
                grad_gain_two,
                grad_shift_two,
            ]
        ),
        ("dp", "tensor"),
        scatter_dimension=1,
        tiled=True,
    )
    return (
        layer_output,
        input_grad,
        owned_attention[0],
        owned_attention[1],
        owned_attention[2],
        owned_attention[3],
        owned_attention[4],
        owned_attention[5],
        owned_vectors[0],
        owned_vectors[1],
        owned_vectors[2],
        owned_feed[0],
        owned_feed[1],
        owned_feed[2],
        owned_vectors[3],
        owned_vectors[4],
        owned_vectors[5],
    )


def solution(mesh):
    placed = (
        P(("dp", "tensor"), None),
        P("dp"),
        P("dp", "tensor"),
        P("dp", "tensor"),
        P("dp", "tensor"),
        P("tensor", "dp"),
        P("tensor", "dp"),
        P("tensor", "dp"),
        P(("dp", "tensor")),
        P(("dp", "tensor")),
        P(("dp", "tensor")),
        P("dp", "tensor"),
        P("tensor", "dp"),
        P("tensor", "dp"),
        P(("dp", "tensor")),
        P(("dp", "tensor")),
        P(("dp", "tensor")),
        P(("dp", "tensor"), None),
    )
    return jax.shard_map(
        body,
        mesh=mesh,
        in_specs=placed,
        out_specs=(
            P(("dp", "tensor"), None),
            P(("dp", "tensor"), None),
            P("dp", "tensor"),
            P("dp", "tensor"),
            P("dp", "tensor"),
            P("tensor", "dp"),
            P("tensor", "dp"),
            P("tensor", "dp"),
            P(("dp", "tensor")),
            P(("dp", "tensor")),
            P(("dp", "tensor")),
            P("dp", "tensor"),
            P("tensor", "dp"),
            P("tensor", "dp"),
            P(("dp", "tensor")),
            P(("dp", "tensor")),
            P(("dp", "tensor")),
        ),
        check_vma=False,
    )
```

profile of v0, /device:TPU:0, one launch (start us, length us, event | category | flops | bytes accessed | tf_op | source)
XLA Modules:
  0.0 1524.9 jit_solution(5309876848612291852)
XLA Ops:
  67.4 26.5 %all-gather.10.cloned.1.call-done = bf16[2048,1024]{1,0:T(8,128)(2,1)} async-done(((bf16[512,1024]{1,0:T(8,128)(2,1)}), bf16[2048,1024]{1,0:T(8,128)(2,1)}) %all-gather.10.cloned.1.call-update) | async-done | bytes 4194320 | tf_op jit(solution)/shard_map/all_gather | solution.py:51
  113.5 129.4 %while.58 = (s32[]{:T(128)}, bf16[4,2048,64]{1,2,0:T(8,128)(2,1)S(1)}, f32[4,2048]{1,0:T(4,128)S(1)}, bf16[4,2048,64]{2,1,0:T(8,128)(2,1)}, bf16[4,2048,64]{2,1,...) while((s32[]{:T(128)}, ...), condition=%wide.region_5.6_spmd.clone, body=%wide.region_0.5_spmd.clone.sunk | while | flops 281026048 | bytes 33902932 | solution.py:116
  116.6 28.6 %while.61 = (s32[]{:T(128)}, bf16[4,512,64]{1,2,0:T(8,128)(2,1)S(1)}, f32[4,512]{1,0:T(4,128)S(1)}, bf16[4,512,64]{2,1,0:T(8,128)(2,1)S(1)}, bf16[2048,64]{1,0:T...) while((s32[]{:T(128)}, ...), condition=%wide.region_4.4_spmd, body=%wide.region_1.3_spmd.sunk | while | flops 281017856 | bytes 30716036 | solution.py:113
  148.9 28.6 %while.61 = (s32[]{:T(128)}, bf16[4,512,64]{1,2,0:T(8,128)(2,1)S(1)}, f32[4,512]{1,0:T(4,128)S(1)}, bf16[4,512,64]{2,1,0:T(8,128)(2,1)S(1)}, bf16[2048,64]{1,0:T...) while((s32[]{:T(128)}, ...), condition=%wide.region_4.4_spmd, body=%wide.region_1.3_spmd.sunk | while | flops 281017856 | bytes 30716036 | solution.py:113
  181.2 28.6 %while.61 = (s32[]{:T(128)}, bf16[4,512,64]{1,2,0:T(8,128)(2,1)S(1)}, f32[4,512]{1,0:T(4,128)S(1)}, bf16[4,512,64]{2,1,0:T(8,128)(2,1)S(1)}, bf16[2048,64]{1,0:T...) while((s32[]{:T(128)}, ...), condition=%wide.region_4.4_spmd, body=%wide.region_1.3_spmd.sunk | while | flops 281017856 | bytes 30716036 | solution.py:113
  213.6 28.6 %while.61 = (s32[]{:T(128)}, bf16[4,512,64]{1,2,0:T(8,128)(2,1)S(1)}, f32[4,512]{1,0:T(4,128)S(1)}, bf16[4,512,64]{2,1,0:T(8,128)(2,1)S(1)}, bf16[2048,64]{1,0:T...) while((s32[]{:T(128)}, ...), condition=%wide.region_4.4_spmd, body=%wide.region_1.3_spmd.sunk | while | flops 281017856 | bytes 30716036 | solution.py:113
  248.2 70.9 %all-gather.2 = f32[32,32,6]{1,2,0:T(8,128)S(1)} all-gather(f32[1,32,6]{1,2,0:T(8,128)S(1)} %bitcast.262), channel_id=1, replica_groups=mesh['dp'=8,'tensor'=4] {'dp','tensor'}, dimensions={0}, use_global_device_ids=true | all-gather | bytes 25344 | tf_op jit(solution)/shard_map/all_gather | solution.py:198
  319.2 73.8 %reduce-scatter.17.cloned.1.call-done = f32[512,1024]{1,0:T(8,128)} async-done(((f32[2048,1024]{1,0:T(8,128)}), f32[512,1024]{1,0:T(8,128)}) %reduce-scatter.17.cloned.1.call-update) | async-done | bytes 2097168 | tf_op jit(solution)/shard_map/reduce_scatter | solution.py:55
  406.5 71.5 %all-gather.12.cloned.1.call-done = bf16[2048,1024]{1,0:T(8,128)(2,1)} async-done(((bf16[512,1024]{1,0:T(8,128)(2,1)}), bf16[2048,1024]{1,0:T(8,128)(2,1)}) %all-gather.12.cloned.1.call-update) | async-done | bytes 4194320 | tf_op jit(solution)/shard_map/all_gather | solution.py:51
  478.0 26.2 %multiply_convert_fusion.1 = (bf16[2048,1024]{1,0:T(8,128)(2,1)}, f32[2048,1024]{1,0:T(8,128)}, f32[2048,1024]{1,0:T(8,128)}) fusion(f32[1024]{0:T(1024)S(1)} %reshape.194, bf16[2048,1024]{1,0:T(8,128)(2,1)} %all-gather.12.cloned.1.call-done, bf16[1024,1024]{1,0:T(8,128)(2,1)} %all-gather.14.cloned.1.call-done), kind=kOutput, calls=%fused_computation.60 | convolution fusion | flops 4433379328 | bytes 27267072 | tf_op jit(solution)/shard_map/dot_general | solution.py:26
  517.6 144.0 %reduce-scatter.19.cloned.1.call-done = f32[512,1024]{1,0:T(8,128)} async-done(((f32[2048,1024]{1,0:T(8,128)}), f32[512,1024]{1,0:T(8,128)}) %reduce-scatter.19.cloned.1.call-update) | async-done | bytes 2097168 | tf_op jit(solution)/shard_map/reduce_scatter | solution.py:55
  668.6 81.0 %all-gather.18.cloned.1.call-done = bf16[2048,1024]{1,0:T(8,128)(2,1)} async-done(((bf16[512,1024]{1,0:T(8,128)(2,1)}), bf16[2048,1024]{1,0:T(8,128)(2,1)}) %all-gather.18.cloned.1.call-update) | async-done | bytes 4194320 | tf_op jit(solution)/shard_map/all_gather | solution.py:59
  772.0 75.4 %reduce-scatter.21.cloned.1.call-done = bf16[512,1024]{1,0:T(8,128)(2,1)} async-done(((bf16[2048,1024]{1,0:T(8,128)(2,1)}), bf16[512,1024]{1,0:T(8,128)(2,1)}) %reduce-scatter.21.cloned.1.call-update) | async-done | bytes 1048592 | tf_op jit(solution)/shard_map/reduce_scatter | solution.py:63
  855.3 79.8 %all-gather.20.cloned.1.call-done = bf16[2048,1024]{1,0:T(8,128)(2,1)} async-done(((bf16[512,1024]{1,0:T(8,128)(2,1)}), bf16[2048,1024]{1,0:T(8,128)(2,1)}) %all-gather.20.cloned.1.call-update) | async-done | bytes 4194320 | tf_op jit(solution)/shard_map/all_gather | solution.py:59
  940.3 230.7 %while.60 = (s32[]{:T(128)}, bf16[4,2048,64]{1,2,0:T(8,128)(2,1)}, bf16[4,2048,64]{1,2,0:T(8,128)(2,1)}, bf16[4,2048,64]{1,2,0:T(8,128)(2,1)}, bf16[4,2048,64]{2...) while((s32[]{:T(128)}, bf16[4,2048,64]{1,2,0:T(8,128)(2,1)}, ...), condition=%wide.region_21.22_spmd.clone, body=%wide.region_17.21_spmd.clone.sunk | while | flops 682401280 | bytes 74053560 | solution.py:157
  944.6 48.6 %while.62 = (s32[]{:T(128)}, f32[2048,64]{0,1:T(8,128)}, f32[2048,64]{0,1:T(8,128)}, bf16[4,512,64]{1,2,0:T(8,128)(2,1)S(1)}, bf16[4,512,64]{2,1,0:T(8,128)(2,1)...) while((s32[]{:T(128)}, f32[2048,64]{0,1:T(8,128)}, ...), condition=%wide.region_20.20_spmd.clone, body=%wide.region_18.19_spmd.clone.sunk | while | flops 682130944 | bytes 68767928 | solution.py:150
  1002.3 48.6 %while.62 = (s32[]{:T(128)}, f32[2048,64]{0,1:T(8,128)}, f32[2048,64]{0,1:T(8,128)}, bf16[4,512,64]{1,2,0:T(8,128)(2,1)S(1)}, bf16[4,512,64]{2,1,0:T(8,128)(2,1)...) while((s32[]{:T(128)}, f32[2048,64]{0,1:T(8,128)}, ...), condition=%wide.region_20.20_spmd.clone, body=%wide.region_18.19_spmd.clone.sunk | while | flops 682130944 | bytes 68767928 | solution.py:150
  1059.9 48.6 %while.62 = (s32[]{:T(128)}, f32[2048,64]{0,1:T(8,128)}, f32[2048,64]{0,1:T(8,128)}, bf16[4,512,64]{1,2,0:T(8,128)(2,1)S(1)}, bf16[4,512,64]{2,1,0:T(8,128)(2,1)...) while((s32[]{:T(128)}, f32[2048,64]{0,1:T(8,128)}, ...), condition=%wide.region_20.20_spmd.clone, body=%wide.region_18.19_spmd.clone.sunk | while | flops 682130944 | bytes 68767928 | solution.py:150
  1117.6 48.6 %while.62 = (s32[]{:T(128)}, f32[2048,64]{0,1:T(8,128)}, f32[2048,64]{0,1:T(8,128)}, bf16[4,512,64]{1,2,0:T(8,128)(2,1)S(1)}, bf16[4,512,64]{2,1,0:T(8,128)(2,1)...) while((s32[]{:T(128)}, f32[2048,64]{0,1:T(8,128)}, ...), condition=%wide.region_20.20_spmd.clone, body=%wide.region_18.19_spmd.clone.sunk | while | flops 682130944 | bytes 68767928 | solution.py:150
  1255.7 32.7 %reduce-scatter.29.cloned.1.call-done = f32[128,256]{0,1:T(8,128)} async-done(((f32[1024,256]{0,1:T(8,128)}), f32[128,256]{0,1:T(8,128)}) %reduce-scatter.29.cloned.1.call-update) | async-done | bytes 131088 | tf_op jit(solution)/shard_map/reduce_scatter | solution.py:273
  1290.1 77.4 %reduce-scatter.23.cloned.1.call-done = bf16[512,1024]{1,0:T(8,128)(2,1)} async-done(((bf16[2048,1024]{1,0:T(8,128)(2,1)}), bf16[512,1024]{1,0:T(8,128)(2,1)}) %reduce-scatter.23.cloned.1.call-update) | async-done | bytes 1048592 | tf_op jit(solution)/shard_map/reduce_scatter | solution.py:63
  1370.3 52.4 %reduce-scatter.35.cloned.1.call-done = f32[1024,128]{1,0:T(8,128)} async-done(((f32[1024,1024]{1,0:T(8,128)}), f32[1024,128]{1,0:T(8,128)}) %reduce-scatter.35.cloned.1.call-update) | async-done | bytes 524304 | tf_op jit(solution)/shard_map/reduce_scatter | solution.py:279
  1422.7 55.0 %reduce-scatter.33.cloned.1.call-done = f32[128,1024]{1,0:T(8,128)} async-done(((f32[1024,1024]{1,0:T(8,128)}), f32[128,1024]{1,0:T(8,128)}) %reduce-scatter.33.cloned.1.call-update) | async-done | bytes 524304 | tf_op jit(solution)/shard_map/reduce_scatter | solution.py:277
  1477.7 39.6 %reduce-scatter.31.cloned.1.call-done = f32[256,128]{1,0:T(8,128)} async-done(((f32[256,1024]{1,0:T(8,128)}), f32[256,128]{1,0:T(8,128)}) %reduce-scatter.31.cloned.1.call-update) | async-done | bytes 131088 | tf_op jit(solution)/shard_map/reduce_scatter | solution.py:276
  (562 shorter events, 599.2 us)
Async XLA Ops:
  8.0 85.9 %all-gather.10.cloned.1.call-start = ((), (), s32[]{:S(2)}) async-start(), calls=%async_computation.11 | async-start | bytes 5242880 | tf_op jit(solution)/shard_map/all_gather | solution.py:51
  8.8 384.2 %reduce-scatter.17.cloned.1.call-start = ((), (), s32[]{:S(2)}) async-start(), calls=%async_computation.12 | async-start | bytes 10485760 | tf_op jit(solution)/shard_map/reduce_scatter | solution.py:55
  37.6 60.7 %copy-start.11 = (bf16[1024,256]{1,0:T(8,128)(2,1)}, bf16[1024,256]{1,0:T(8,128)(2,1)S(1)}, u32[]{:S(2)}) copy-start(bf16[1024,256]{1,0:T(8,128)(2,1)S(1)} %all_gather.52) | copy-start | bytes 1572868
  47.2 53.9 %copy-start.13 = (bf16[1024,256]{1,0:T(8,128)(2,1)}, bf16[1024,256]{1,0:T(8,128)(2,1)S(1)}, u32[]{:S(2)}) copy-start(bf16[1024,256]{1,0:T(8,128)(2,1)S(1)} %all_gather.49) | copy-start | bytes 1572868
  56.3 51.9 %copy-start.15 = (bf16[1024,256]{1,0:T(8,128)(2,1)}, bf16[1024,256]{1,0:T(8,128)(2,1)S(1)}, u32[]{:S(2)}) copy-start(bf16[1024,256]{1,0:T(8,128)(2,1)S(1)} %all_gather.51) | copy-start | bytes 1572868
  113.5 129.4 %copy-start.17 = (bf16[256,1024]{1,0:T(8,128)(2,1)S(1)}, bf16[256,1024]{1,0:T(8,128)(2,1)}, u32[]{:S(2)}) copy-start(bf16[256,1024]{1,0:T(8,128)(2,1)} %all_gather.54) | copy-start | bytes 1572868
  247.5 145.5 %copy-start.9 = (bf16[512,1024]{1,0:T(8,128)(2,1)S(1)}, bf16[512,1024]{1,0:T(8,128)(2,1)}, u32[]{:S(2)}) copy-start(bf16[512,1024]{1,0:T(8,128)(2,1)} %param.26) | copy-start | bytes 3145732
  247.5 159.0 %all-gather.14.cloned.1.call-start = ((), (), s32[]{:S(2)}) async-start(), calls=%async_computation.14 | async-start | bytes 2359296 | tf_op jit(solution)/shard_map/all_gather | solution.py:81
  248.1 230.0 %all-gather.12.cloned.1.call-start = ((), (), s32[]{:S(2)}) async-start(), calls=%async_computation.13 | async-start | bytes 5242880 | tf_op jit(solution)/shard_map/all_gather | solution.py:51
  396.7 109.6 %all-gather.16.cloned.1.call-start = ((), (), s32[]{:S(2)}) async-start(), calls=%async_computation.15 | async-start | bytes 2359296 | tf_op jit(solution)/shard_map/all_gather | solution.py:83
  397.3 264.4 %reduce-scatter.19.cloned.1.call-start = ((), (), s32[]{:S(2)}) async-start(), calls=%async_computation.16 | async-start | bytes 10485760 | tf_op jit(solution)/shard_map/reduce_scatter | solution.py:55
  516.9 232.7 %all-gather.18.cloned.1.call-start = ((), (), s32[]{:S(2)}) async-start(), calls=%async_computation.17 | async-start | bytes 5242880 | tf_op jit(solution)/shard_map/all_gather | solution.py:59
  668.2 179.2 %reduce-scatter.21.cloned.1.call-start = ((), (), s32[]{:S(2)}) async-start(), calls=%async_computation.18 | async-start | bytes 5242880 | tf_op jit(solution)/shard_map/reduce_scatter | solution.py:63
  772.0 163.1 %all-gather.20.cloned.1.call-start = ((), (), s32[]{:S(2)}) async-start(), calls=%async_computation.19 | async-start | bytes 5242880 | tf_op jit(solution)/shard_map/all_gather | solution.py:59
  851.4 83.7 %copy-start.18 = (bf16[256,1024]{1,0:T(8,128)(2,1)S(1)}, bf16[256,1024]{1,0:T(8,128)(2,1)}, u32[]{:S(2)}) copy-start(bf16[256,1024]{1,0:T(8,128)(2,1)} %all_gather.54) | copy-start | bytes 1572868
  853.8 366.1 %reduce-scatter.37.cloned.1.call-start = ((), (), s32[]{:S(2)}) async-start(), calls=%async_computation.27 | async-start | bytes 540672
  855.0 397.4 %reduce-scatter.25.cloned.1.call-start = ((), (), s32[]{:S(2)}) async-start(), calls=%async_computation.21 | async-start | bytes 1179648 | tf_op jit(solution)/shard_map/reduce_scatter | solution.py:271
  1175.8 78.2 %reduce-scatter.27.cloned.1.call-start = ((), (), s32[]{:S(2)}) async-start(), calls=%async_computation.22 | async-start | bytes 1179648 | tf_op jit(solution)/shard_map/reduce_scatter | solution.py:272
  1180.5 108.0 %reduce-scatter.29.cloned.1.call-start = ((), (), s32[]{:S(2)}) async-start(), calls=%async_computation.23 | async-start | bytes 1179648 | tf_op jit(solution)/shard_map/reduce_scatter | solution.py:273
  1185.2 182.3 %reduce-scatter.23.cloned.1.call-start = ((), (), s32[]{:S(2)}) async-start(), calls=%async_computation.20 | async-start | bytes 5242880 | tf_op jit(solution)/shard_map/reduce_scatter | solution.py:63
  1193.0 229.7 %reduce-scatter.35.cloned.1.call-start = ((), (), s32[]{:S(2)}) async-start(), calls=%async_computation.26 | async-start | bytes 4718592 | tf_op jit(solution)/shard_map/reduce_scatter | solution.py:279
  1203.2 274.4 %reduce-scatter.33.cloned.1.call-start = ((), (), s32[]{:S(2)}) async-start(), calls=%async_computation.25 | async-start | bytes 4718592 | tf_op jit(solution)/shard_map/reduce_scatter | solution.py:277
  1213.7 153.8 %copy-start.4 = (f32[512,1024]{1,0:T(8,128)S(1)}, f32[512,1024]{1,0:T(8,128)}, u32[]{:S(2)}) copy-start(f32[512,1024]{1,0:T(8,128)} %copy-done.3) | copy-start | bytes 6291460
  1213.7 303.6 %reduce-scatter.31.cloned.1.call-start = ((), (), s32[]{:S(2)}) async-start(), calls=%async_computation.24 | async-start | bytes 1179648 | tf_op jit(solution)/shard_map/reduce_scatter | solution.py:276
  (70 other events, 188.2 us)
Sparse Core Ops, SparseCore 0:
  10.4 83.4 all-gather.9
  247.6 145.3 reduce-scatter.16
  668.3 81.2 all-gather.17
  772.1 75.2 reduce-scatter.20
Sparse Core Ops, SparseCore 1:
  249.9 26.2 all-gather.13
  396.8 81.2 all-gather.11
  479.8 26.4 all-gather.15
  517.0 144.6 reduce-scatter.18
  853.9 81.1 all-gather.19
  937.3 134.6 reduce-scatter.36
  1175.9 34.4 reduce-scatter.24
  1213.4 36.0 reduce-scatter.26
  1252.5 35.9 reduce-scatter.28
  1290.7 76.7 reduce-scatter.22
  1371.3 51.4 reduce-scatter.34
  1426.7 51.0 reduce-scatter.32
  1481.3 35.9 reduce-scatter.30
where the time goes:
time: 1530 us; the launch traced here: 1520 us
  waiting for transfers between devices  813 us (53%)
  matrix products  344 us (22%)
  blocking collectives  162 us (11%)
  local copies, waits for them, and re-layouts  121 us (8%)
  other arithmetic  62.9 us (4%)
  between operations  17.7 us (1%)
    reduce_scatter x2, waiting for transfers between devices, scatter_sequence(): lax.psum_scatter(partial_sum, 'tensor', scatter_dimension=0, tiled=True)  218 us
    all_gather x2, waiting for transfers between devices, gather_gradient(): return lax.all_gather(local_rows, 'tensor', axis=0, tiled=True)  161 us
    reduce_scatter x2, waiting for transfers between devices, scatter_gradient(): lax.psum_scatter(partial_sum.astype(jnp.bfloat16), 'tensor', scatter_dime...  153 us
    dot_general x38, matrix products, plain_product(): return jnp.dot(left, right, preferred_element_type=jnp.float32)  120 us
    dot_general x38, matrix products, contract_rows(): lax.dot_general(left, right, (((0,), (0,)), ((), ())), preferred_element_...  118 us
    dot_general x54, matrix products, contract_cols(): lax.dot_general(left, right, (((1,), (1,)), ((), ())), preferred_element_...  106 us
    all_gather x2, waiting for transfers between devices, gather_sequence(): return lax.all_gather(local_rows, 'tensor', axis=0, tiled=True)  98 us
    all_gather x1, blocking collectives, body(): lax.all_gather(jnp.stack([output_bias, first_gain, first_shift, outer_bia...  70.9 us
  transfers between devices with their start and end apart: 17, of which 13 were waited for; matrix products, arithmetic and copies ran while one was open for 20% of the time, Pallas kernels for 0%

commit v1 on v0

v1 whole, which is shorter than its diff:
```python
import jax
import jax.numpy as jnp
from jax import lax
from jax.experimental import pallas as pl
from jax.experimental.pallas import tpu as pltpu
from jax.sharding import PartitionSpec as P

HEAD_DIM = 64


EPSILON = 1e-12
NEG_LARGE = 1000000000.0


def contract_rows(left, right):
    return lax.dot_general(
        left, right, (((0,), (0,)), ((), ())), preferred_element_type=jnp.float32
    )


def contract_cols(left, right):
    return lax.dot_general(
        left, right, (((1,), (1,)), ((), ())), preferred_element_type=jnp.float32
    )


def plain_product(left, right):
    return jnp.dot(left, right, preferred_element_type=jnp.float32)


def gelu_exact(value):
    return jax.nn.gelu(value, approximate=False)


def norm_forward(hidden, gain, shift):
    center = hidden - jnp.mean(hidden, -1, keepdims=True)
    inverse = lax.rsqrt(jnp.mean(center * center, -1, keepdims=True) + EPSILON)
    normed = center * inverse
    return (normed * gain + shift, normed, inverse)


def norm_backward(grad_out, normed, inverse, gain):
    grad_norm = grad_out * gain
    grad_hidden = inverse * (
        grad_norm
        - jnp.mean(grad_norm, -1, keepdims=True)
        - normed * jnp.mean(grad_norm * normed, -1, keepdims=True)
    )
    return (grad_hidden, jnp.sum(grad_out * normed, 0), jnp.sum(grad_out, 0))


LANES = 128
SCALE = HEAD_DIM ** (-0.5)
EVERY = ("tensor", "dp")


def lane_index(shape):
    return lax.broadcasted_iota(jnp.int32, shape, 1)


def in_half(lane, half):
    return (lane >= half * HEAD_DIM) & (lane < (half + 1) * HEAD_DIM)


def split_three(value):
    first = value.astype(jnp.bfloat16).astype(jnp.float32)
    second = (value - first).astype(jnp.bfloat16).astype(jnp.float32)
    third = (value - first - second).astype(jnp.bfloat16).astype(jnp.float32)
    return (first, second, third)


def key_bias_column(length, rows):
    position = lax.broadcasted_iota(jnp.int32, (rows, LANES), 0)
    return jnp.where(position < length, 0.0, -NEG_LARGE)


def forward_kernel(length_ref, q_ref, k_ref, v_ref, context_ref, logsum_ref, key_aug, value_aug):
    rows, seq_len = (q_ref.shape[0], k_ref.shape[0])

    @pl.when(pl.program_id(1) == 0)
    def prepare():
        lane = lane_index((seq_len, LANES))
        bias = key_bias_column(length_ref[0], seq_len)
        keys = k_ref[...].astype(jnp.float32)
        values = v_ref[...].astype(jnp.float32)
        for half in range(2):
            own = in_half(lane, half)
            spare = HEAD_DIM * (1 - half)
            key_aug[half] = jnp.where(
                own, keys, jnp.where(lane == spare, bias, 0.0)
            ).astype(jnp.bfloat16)
            value_aug[half] = jnp.where(
                own, values, jnp.where(lane == spare, 1.0, 0.0)
            ).astype(jnp.bfloat16)

    lane = lane_index((rows, LANES))
    queries = q_ref[...].astype(jnp.float32) * SCALE
    contexts, logsums = ([], [])
    for half in range(2):
        own = in_half(lane, half)
        spare = HEAD_DIM * (1 - half)
        query = jnp.where(own, queries, jnp.where(lane == spare, 1.0, 0.0)).astype(jnp.bfloat16)
        scores = contract_cols(query, key_aug[half])
        highest = jnp.max(scores, -1, keepdims=True)
        weights = jnp.exp(scores - highest).astype(jnp.bfloat16)
        summed = plain_product(weights, value_aug[half])
        totals = summed[:, spare : spare + 1]
        contexts.append(summed / totals)
        logsums.append(highest + jnp.log(totals))
    first = in_half(lane, 0)
    context_ref[...] = jnp.where(first, contexts[0], contexts[1]).astype(jnp.bfloat16)
    logsum_ref[...] = jnp.where(first, logsums[0], logsums[1])


def backward_kernel(
    length_ref,
    q_ref,
    k_ref,
    v_ref,
    context_ref,
    logsum_ref,
    grad_ref,
    dq_ref,
    dk_ref,
    dv_ref,
    key_aug,
    value_aug,
    key_flipped,
    dk_sum,
    dv_sum,
):
    rows, seq_len = (q_ref.shape[0], k_ref.shape[0])
    step = pl.program_id(1)

    @pl.when(step == 0)
    def prepare():
        lane = lane_index((seq_len, LANES))
        bias = key_bias_column(length_ref[0], seq_len)
        keys = k_ref[...].astype(jnp.float32)
        values = v_ref[...].astype(jnp.float32)
        key_flipped[...] = keys.T.astype(jnp.bfloat16)
        for half in range(2):
            own = in_half(lane, half)
            spare = HEAD_DIM * (1 - half)
            after = (lane > spare) & (lane <= spare + 3)
            key_aug[half] = jnp.where(
                own, keys, jnp.where(lane == spare, bias, jnp.where(after, 1.0, 0.0))
            ).astype(jnp.bfloat16)
            value_aug[half] = jnp.where(own, values, jnp.where(after, 1.0, 0.0)).astype(
                jnp.bfloat16
            )
        dk_sum[...] = jnp.zeros_like(dk_sum)
        dv_sum[...] = jnp.zeros_like(dv_sum)

    lane = lane_index((rows, LANES))
    queries = q_ref[...].astype(jnp.float32) * SCALE
    grads = grad_ref[...].astype(jnp.float32)
    product = grads * context_ref[...].astype(jnp.float32)
    logsum_all = logsum_ref[...]
    flipped = []
    for half in range(2):
        own = in_half(lane, half)
        spare = HEAD_DIM * (1 - half)
        delta = jnp.sum(jnp.where(own, product, 0.0), -1, keepdims=True)
        logsum = logsum_all[:, half * HEAD_DIM : half * HEAD_DIM + 1]
        query = jnp.where(own, queries, jnp.where(lane == spare, 1.0, 0.0))
        grad = jnp.where(own, grads, 0.0)
        for place, (less, minus) in enumerate(zip(split_three(-logsum), split_three(-delta))):
            here = lane == spare + 1 + place
            query = jnp.where(here, less, query)
            grad = jnp.where(here, minus, grad)
        query = query.astype(jnp.bfloat16)
        grad = grad.astype(jnp.bfloat16)
        weights = jnp.exp(contract_cols(key_aug[half], query))
        dv_sum[half] += plain_product(weights.astype(jnp.bfloat16), grad)
        grad_scores = (weights * contract_cols(value_aug[half], grad)).astype(jnp.bfloat16)
        dk_sum[half] += plain_product(grad_scores, query)
        flipped.append(
            plain_product(
                key_flipped[half * HEAD_DIM : (half + 1) * HEAD_DIM, :], grad_scores
            )
        )
    dq_ref[...] = (jnp.concatenate(flipped, 0).T * SCALE).astype(jnp.bfloat16)

    @pl.when(step == pl.num_programs(1) - 1)
    def finish():
        first = in_half(lane_index((seq_len, LANES)), 0)
        dk_ref[...] = jnp.where(first, dk_sum[0], dk_sum[1]).astype(jnp.bfloat16)
        dv_ref[...] = jnp.where(first, dv_sum[0], dv_sum[1]).astype(jnp.bfloat16)


def attend_forward(qkv_rows, lengths):
    seq_len, columns = qkv_rows.shape
    width = columns // 3
    pairs = width // LANES
    rows = min(512, seq_len)
    block = pl.BlockSpec((rows, LANES), lambda pair, step: (step, pair))
    return pl.pallas_call(
        forward_kernel,
        grid=(pairs, seq_len // rows),
        in_specs=[
            pl.BlockSpec(memory_space=pltpu.SMEM),
            block,
            pl.BlockSpec((seq_len, LANES), lambda pair, step: (0, pairs + pair)),
            pl.BlockSpec((seq_len, LANES), lambda pair, step: (0, 2 * pairs + pair)),
        ],
        out_specs=[block, block],
        out_shape=[
            jax.ShapeDtypeStruct((seq_len, width), jnp.bfloat16),
            jax.ShapeDtypeStruct((seq_len, width), jnp.float32),
        ],
        scratch_shapes=[pltpu.VMEM((2, seq_len, LANES), jnp.bfloat16)] * 2,
        compiler_params=pltpu.CompilerParams(vmem_limit_bytes=48 * 2**20),
        cost_estimate=pl.CostEstimate(
            flops=16 * seq_len * seq_len * width,
            bytes_accessed=10 * seq_len * width,
            transcendentals=seq_len * seq_len * width // HEAD_DIM,
        ),
        name="attend_forward",
    )(lengths, qkv_rows, qkv_rows, qkv_rows)


def attend_backward(qkv_rows, lengths, context, logsum, grad_context):
    seq_len, columns = qkv_rows.shape
    width = columns // 3
    pairs = width // LANES
    rows = min(256, seq_len)
    block = pl.BlockSpec((rows, LANES), lambda pair, step: (step, pair))
    whole = pl.BlockSpec((seq_len, LANES), lambda pair, step: (0, pair))
    return pl.pallas_call(
        backward_kernel,
        grid=(pairs, seq_len // rows),
        in_specs=[
            pl.BlockSpec(memory_space=pltpu.SMEM),
            block,
            pl.BlockSpec((seq_len, LANES), lambda pair, step: (0, pairs + pair)),
            pl.BlockSpec((seq_len, LANES), lambda pair, step: (0, 2 * pairs + pair)),
            block,
            block,
            block,
        ],
        out_specs=[block, whole, whole],
        out_shape=[jax.ShapeDtypeStruct((seq_len, width), jnp.bfloat16)] * 3,
        scratch_shapes=[
            pltpu.VMEM((2, seq_len, LANES), jnp.bfloat16),
            pltpu.VMEM((2, seq_len, LANES), jnp.bfloat16),
            pltpu.VMEM((LANES, seq_len), jnp.bfloat16),
            pltpu.VMEM((2, seq_len, LANES), jnp.float32),
            pltpu.VMEM((2, seq_len, LANES), jnp.float32),
        ],
        compiler_params=pltpu.CompilerParams(vmem_limit_bytes=48 * 2**20),
        cost_estimate=pl.CostEstimate(
            flops=40 * seq_len * seq_len * width,
            bytes_accessed=20 * seq_len * width,
            transcendentals=seq_len * seq_len * width // HEAD_DIM,
        ),
        name="attend_backward",
    )(lengths, qkv_rows, qkv_rows, qkv_rows, context, logsum, grad_context)


def gather_everywhere(block):
    whole = lax.all_gather(block, EVERY, axis=0, tiled=True)
    return whole.reshape(lax.axis_size("tensor"), -1, block.shape[1])


def scatter_everywhere(blocks):
    rows = lax.axis_size("dp")
    columns = blocks[0].shape[1]
    stacked = jnp.stack([block.reshape(rows, -1, columns) for block in blocks], 1)
    summed = lax.psum_scatter(
        stacked.reshape(-1, columns), "dp", scatter_dimension=0, tiled=True
    )
    return lax.psum_scatter(summed, "tensor", scatter_dimension=0, tiled=True).astype(
        jnp.float32
    )


def exchange(blocks):
    return lax.all_to_all(blocks, "tensor", split_axis=0, concat_axis=0, tiled=True)


def pack_owned(whole, own_shape):
    parts = whole.reshape(whole.shape[0], own_shape[0], -1, own_shape[1])
    return parts.transpose(2, 0, 1, 3).reshape(parts.shape[2], whole.shape[0], -1)


def unpack_owned(pieces, own_shape):
    parts = pieces.reshape(pieces.shape[0], pieces.shape[1], own_shape[0], own_shape[1])
    return parts.transpose(1, 2, 0, 3).reshape(pieces.shape[1], -1)


def body(
    inputs,
    lengths,
    query_weight,
    key_weight,
    value_weight,
    query_bias,
    value_bias,
    output_weight,
    output_bias,
    first_gain,
    first_shift,
    inner_weight,
    inner_bias,
    outer_weight,
    outer_bias,
    second_gain,
    second_shift,
    cotangent,
):
    low = jnp.bfloat16
    local_rows, model = inputs.shape
    tensor_size = lax.axis_size("tensor")
    dp_size = lax.axis_size("dp")
    place = lax.axis_index("tensor")
    positions = jnp.arange(local_rows, dtype=jnp.int32) + place * local_rows
    valid_mine = (positions < lengths[0]).astype(jnp.float32)[:, None]

    small = [query_bias, value_bias, inner_bias]
    vectors = [output_bias, first_gain, first_shift, outer_bias, second_gain, second_shift]
    packed = jnp.concatenate([part.reshape(-1).astype(jnp.float32) for part in small + vectors])
    packed = lax.all_gather(packed[None], ("dp", "tensor"), axis=0, tiled=True)
    packed = packed.reshape(dp_size, tensor_size, -1)
    cut_one = query_bias.size
    cut_two = cut_one + value_bias.size
    cut_three = cut_two + inner_bias.size
    bias_query = unpack_owned(packed[:, :, :cut_one], query_bias.shape)
    bias_value = unpack_owned(packed[:, :, cut_one:cut_two], value_bias.shape)
    bias_inner = unpack_owned(packed[:, :, cut_two:cut_three], inner_bias.shape)
    vectors = packed[:, :, cut_three:].reshape(dp_size * tensor_size, 6, -1)
    vectors = vectors.transpose(1, 0, 2).reshape(6, -1)
    bias_out, gain_one, shift_one, bias_two, gain_two, shift_two = vectors

    width = query_weight.shape[1]
    projections = jnp.concatenate([query_weight, key_weight, value_weight], 1)
    full_projection = lax.all_gather(projections, "dp", axis=0, tiled=True)
    seq_inputs = lax.all_gather(inputs, "tensor", axis=0, tiled=True)
    full_output = gather_everywhere(output_weight.T)
    full_inner = gather_everywhere(inner_weight)
    full_outer = gather_everywhere(outer_weight.T)
    bias_qkv = jnp.concatenate(
        [bias_query[place], jnp.zeros((width,), jnp.float32), bias_value[place]]
    )
    qkv_rows = (plain_product(seq_inputs, full_projection) + bias_qkv).astype(low)
    context, logsum = attend_forward(qkv_rows, lengths)
    context_mine = exchange(context.reshape(tensor_size, local_rows, width))
    attention_mine = sum(
        contract_cols(context_mine[t], full_output[t]) for t in range(tensor_size)
    )
    hidden_one = inputs.astype(jnp.float32) + attention_mine + bias_out
    middle, normed_one, inverse_one = norm_forward(hidden_one, gain_one, shift_one)
    middle_low = middle.astype(low)
    pre_act = [
        plain_product(middle_low, full_inner[t]) + bias_inner[t] for t in range(tensor_size)
    ]
    act_low = [gelu_exact(part).astype(low) for part in pre_act]
    mlp_mine = sum(contract_cols(act_low[t], full_outer[t]) for t in range(tensor_size))
    hidden_two = middle + mlp_mine + bias_two
    final, normed_two, inverse_two = norm_forward(hidden_two, gain_two, shift_two)
    layer_output = (final * valid_mine).astype(low)

    grad_final = cotangent.astype(jnp.float32) * valid_mine
    grad_two, grad_gain_two, grad_shift_two = norm_backward(
        grad_final, normed_two, inverse_two, gain_two
    )
    grad_bias_two = jnp.sum(grad_two, 0)
    grad_two_low = grad_two.astype(low)
    owned_outer = scatter_everywhere(
        [contract_rows(grad_two_low, part).astype(low) for part in act_low]
    ).T
    grad_pre = []
    for t in range(tensor_size):
        grad_act = plain_product(grad_two_low, full_outer[t])
        grad_pre.append(jax.vjp(gelu_exact, pre_act[t])[1](grad_act)[0].astype(low))
    grad_inner_bias = jnp.stack([jnp.sum(part.astype(jnp.float32), 0) for part in grad_pre])
    owned_inner = scatter_everywhere(
        [contract_rows(middle_low, part).astype(low) for part in grad_pre]
    )
    grad_middle = grad_two + sum(
        contract_cols(grad_pre[t], full_inner[t]) for t in range(tensor_size)
    )
    grad_one, grad_gain_one, grad_shift_one = norm_backward(
        grad_middle, normed_one, inverse_one, gain_one
    )
    grad_bias_out = jnp.sum(grad_one, 0)
    grad_one_low = grad_one.astype(low)
    grad_context_mine = jnp.stack(
        [plain_product(grad_one_low, full_output[t]).astype(low) for t in range(tensor_size)]
    )
    owned_output = scatter_everywhere(
        [contract_rows(grad_one_low, context_mine[t]).astype(low) for t in range(tensor_size)]
    ).T
    grad_context = exchange(grad_context_mine).reshape(-1, width)
    grad_vectors = jnp.stack(
        [
            grad_bias_out,
            grad_gain_one,
            grad_shift_one,
            grad_bias_two,
            grad_gain_two,
            grad_shift_two,
        ]
    )
    grad_vectors = grad_vectors.reshape(6, dp_size * tensor_size, -1).transpose(1, 0, 2)
    grad_vectors = grad_vectors.reshape(dp_size * tensor_size, -1)
    grad_small = pack_owned(
        grad_inner_bias.reshape(tensor_size, inner_bias.shape[0], -1), inner_bias.shape
    ).reshape(dp_size * tensor_size, -1)
    owned_early = lax.psum_scatter(
        jnp.concatenate([grad_small, grad_vectors], 1),
        ("dp", "tensor"),
        scatter_dimension=0,
        tiled=True,
    )[0]
    owned_inner_bias = owned_early[: inner_bias.size].reshape(inner_bias.shape)
    owned_vectors = owned_early[inner_bias.size :].reshape(6, -1)

    grad_qkv = jnp.concatenate(
        attend_backward(qkv_rows, lengths, context, logsum, grad_context), 1
    )
    input_part = contract_cols(grad_qkv, full_projection)
    input_grad = grad_one + lax.psum_scatter(
        input_part.astype(low), "tensor", scatter_dimension=0, tiled=True
    ).astype(jnp.float32)
    owned_projection = lax.psum_scatter(
        contract_rows(seq_inputs, grad_qkv).astype(low), "dp", scatter_dimension=0, tiled=True
    ).astype(jnp.float32)
    sums = jnp.sum(grad_qkv.astype(jnp.float32), 0).reshape(1, 3, -1)
    pieces = [
        pack_owned(sums[:, which].reshape(1, query_bias.shape[0], -1), query_bias.shape)
        for which in (0, 2)
    ]
    owned_biases = lax.psum_scatter(
        jnp.concatenate(pieces, 2).reshape(dp_size, -1), "dp", scatter_dimension=0, tiled=True
    )[0]
    return (
        layer_output,
        input_grad,
        owned_projection[:, :width],
        owned_projection[:, width : 2 * width],
        owned_projection[:, 2 * width :],
        owned_biases[:cut_one].reshape(query_bias.shape),
        owned_biases[cut_one:].reshape(value_bias.shape),
        owned_output,
        owned_vectors[0],
        owned_vectors[1],
        owned_vectors[2],
        owned_inner,
        owned_inner_bias,
        owned_outer,
        owned_vectors[3],
        owned_vectors[4],
        owned_vectors[5],
    )


def solution(mesh):
    placed = (
        P(("dp", "tensor"), None),
        P("dp"),
        P("dp", "tensor"),
        P("dp", "tensor"),
        P("dp", "tensor"),
        P("tensor", "dp"),
        P("tensor", "dp"),
        P("tensor", "dp"),
        P(("dp", "tensor")),
        P(("dp", "tensor")),
        P(("dp", "tensor")),
        P("dp", "tensor"),
        P("tensor", "dp"),
        P("tensor", "dp"),
        P(("dp", "tensor")),
        P(("dp", "tensor")),
        P(("dp", "tensor")),
        P(("dp", "tensor"), None),
    )
    return jax.shard_map(
        body,
        mesh=mesh,
        in_specs=placed,
        out_specs=(
            P(("dp", "tensor"), None),
            P(("dp", "tensor"), None),
            P("dp", "tensor"),
            P("dp", "tensor"),
            P("dp", "tensor"),
            P("tensor", "dp"),
            P("tensor", "dp"),
            P("tensor", "dp"),
            P(("dp", "tensor")),
            P(("dp", "tensor")),
            P(("dp", "tensor")),
            P("dp", "tensor"),
            P("tensor", "dp"),
            P("tensor", "dp"),
            P(("dp", "tensor")),
            P(("dp", "tensor")),
            P(("dp", "tensor")),
        ),
        check_vma=False,
    )
```

time: 1530 us -> 827 us (0.54)
  waiting for transfers between devices: 813 us -> 350 us
  matrix products: 344 us -> 101 us
  Pallas kernels: 0 us -> 85.4 us
  local copies, waits for them, and re-layouts: 121 us -> 81.8 us
  other arithmetic: 62.9 us -> 26.3 us
    reduce_scatter x10 -> x5, waiting for transfers between devices: 550 us -> 122 us  [the longest x1 75.8 us: body(): lax.psum_scatter(input_part.astype(low), 'tensor', scatter_dimension=0, t...]
    dot_general x38 -> x13, matrix products: 118 us -> 19.4 us  [contract_rows(): lax.dot_general(left, right, (((0,), (0,)), ((), ())), preferred_element_...]
    pallas_call x0 -> x2, Pallas kernels: none -> 85.4 us  [the longest x1 52.6 us: attend_backward(): pl.pallas_call(backward_kernel, grid=(pairs, seq_len // rows), in_specs=[...]
    dot_general x54 -> x13, matrix products: 106 us -> 26.6 us  [contract_cols(): lax.dot_general(left, right, (((1,), (1,)), ((), ())), preferred_element_...]
    all_gather x6 -> x5, waiting for transfers between devices: 261 us -> 183 us  [the longest x3 148 us: gather_everywhere(): whole = lax.all_gather(block, EVERY, axis=0, tiled=True)]
    all_gather x8 -> x1, blocking collectives: 138 us -> 72.2 us  [body(): packed = lax.all_gather(packed[None], ('dp', 'tensor'), axis=0, tiled=True)]
    dot_general x38 -> x13, matrix products: 120 us -> 54.9 us  [plain_product(): return jnp.dot(left, right, preferred_element_type=jnp.float32)]
    while x108 -> x0, local copies, waits for them, and re-layouts: 64.9 us -> none
  transfers between devices with their start and end apart: 17 -> 14, of which waited for: 13 -> 10; matrix products, arithmetic and copies ran while one was open for 20% -> 16% of each run, Pallas kernels for 0% -> 10%
where the time goes in v1:
time: 827 us; the launch traced here: 819 us
  waiting for transfers between devices  350 us (42%)
  blocking collectives  154 us (19%)
  matrix products  101 us (12%)
  Pallas kernels  85.4 us (10%)
  local copies, waits for them, and re-layouts  81.8 us (10%)
  other arithmetic  26.3 us (3%)
  between operations  15.9 us (2%)
    all_gather x3, waiting for transfers between devices, gather_everywhere(): whole = lax.all_gather(block, EVERY, axis=0, tiled=True)  148 us
    reduce_scatter x1, waiting for transfers between devices, body(): lax.psum_scatter(input_part.astype(low), 'tensor', scatter_dimension=0, t...  75.8 us
    all_gather x1, blocking collectives, body(): packed = lax.all_gather(packed[None], ('dp', 'tensor'), axis=0, tiled=True)  72.2 us
    dot_general x13, matrix products, plain_product(): return jnp.dot(left, right, preferred_element_type=jnp.float32)  54.9 us
    unnamed x2, blocking collectives  52.7 us
    pallas_call x1, Pallas kernels, attend_backward(): pl.pallas_call(backward_kernel, grid=(pairs, seq_len // rows), in_specs=[...  52.6 us
    all_gather x1, waiting for transfers between devices, body(): seq_inputs = lax.all_gather(inputs, 'tensor', axis=0, tiled=True)  35.7 us
    pallas_call x1, Pallas kernels, attend_forward(): pl.pallas_call(forward_kernel, grid=(pairs, seq_len // rows), in_specs=[p...  32.7 us
  transfers between devices with their start and end apart: 14, of which 10 were waited for; matrix products, arithmetic and copies ran while one was open for 16% of the time, Pallas kernels for 10%

profile of v1, /device:TPU:0, one launch (start us, length us, event | category | flops | bytes accessed | tf_op | source)
XLA Modules:
  0.0 818.6 jit_solution(4670024434794583423)
XLA Ops:
  12.8 72.2 %all-gather.1 = f32[32,1,384]{2,1,0:T(1,128)S(1)} all-gather(f32[1,1,384]{2,1,0:T(1,128)S(1)} %reshape.266), channel_id=2, replica_groups=mesh['dp'=8,'tensor'=4] {'dp','tensor'}, dimensions={0}, use_global_device_ids=true | all-gather | bytes 50688 | tf_op jit(solution)/shard_map/all_gather | solution.py:323
  85.7 35.7 %all-gather.10.cloned.1.call-done = bf16[2048,1024]{1,0:T(8,128)(2,1)} async-done(((bf16[512,1024]{1,0:T(8,128)(2,1)}), bf16[2048,1024]{1,0:T(8,128)(2,1)}) %all-gather.10.cloned.1.call-update) | async-done | bytes 4194320 | tf_op jit(solution)/shard_map/all_gather | solution.py:338
  121.5 7.9 fusion.q_ref.k_ref.v_ref
  129.3 32.7 %attend_forward.1 = (bf16[2048,256]{1,0:T(8,128)(2,1)}, f32[2048,256]{1,0:T(8,128)S(1)}) custom-call(s32[1]{0:T(128)} %copy.113.length_ref, bf16[2048,768]{1,0:T(8,128)(2,1)} %fusion.q_ref.k_ref.v_ref, bf16[2048,768]{1,0:T(8,128)(2,1)} %fusion.q_ref.k_ref.v_ref, bf16[2048,768]{1,0:T(8,128)(2,1)} %fusion.q_ref.k_ref.v_ref), custom_call_target="tpu_custom_call" | custom-call | flops 17179869184 | bytes 5242880 | tf_op jit(solution)/shard_map/attend_forward/pallas_call | solution.py:198
  169.1 13.7 %all-gather.12.cloned.1.call-done = bf16[4096,256]{0,1:T(8,128)(2,1)} async-done(((bf16[128,256]{0,1:T(8,128)(2,1)}), bf16[4096,256]{0,1:T(8,128)(2,1)}) %all-gather.12.cloned.1.call-update) | async-done | bytes 2097168 | tf_op jit(solution)/shard_map/all_gather | solution.py:262
  182.8 12.8 %all-to-all-done = bf16[4,512,256]{2,1,0:T(8,128)(2,1)S(1)} async-done(((bf16[4,512,256]{2,1,0:T(8,128)(2,1)}), bf16[4,512,256]{2,1,0:T(8,128)(2,1)S(1)}, u32[]{:S(2)}, u32[]{:S(2)}) %all-to-all-start) | async-done | bytes 1048608 | tf_op jit(solution)/shard_map/all_to_all | solution.py:279
  202.5 58.1 %all-gather.14.cloned.1.call-done = bf16[4096,1024]{1,0:T(8,128)(2,1)} async-done(((bf16[128,1024]{1,0:T(8,128)(2,1)}), bf16[4096,1024]{1,0:T(8,128)(2,1)}) %all-gather.14.cloned.1.call-update) | async-done | bytes 8388624 | tf_op jit(solution)/shard_map/all_gather | solution.py:262
  260.5 8.9 %multiply_convert_fusion.1 = (bf16[512,1024]{1,0:T(8,128)(2,1)}, f32[512,1024]{1,0:T(8,128)}, f32[512,1024]{1,0:T(8,128)}) fusion(f32[1024]{0:T(1024)S(1)} %add.203, bf16[512,1024]{1,0:T(8,128)(2,1)} %fusion.28, bf16[4096,1024]{1,0:T(8,128)(2,1)} %all-gather.14.cloned.1.call-done), kind=kOutput, calls=%fused_computation.38 | convolution fusion | flops 1108344832 | bytes 8392704 | tf_op jit(solution)/shard_map/dot_general | solution.py:28
  269.4 8.4 %multiply_convert_fusion.2 = (bf16[512,1024]{1,0:T(8,128)(2,1)}, f32[512,1024]{1,0:T(8,128)}, f32[512,1024]{1,0:T(8,128)}) fusion(f32[1024]{0:T(1024)S(1)} %add.199, bf16[512,1024]{1,0:T(8,128)(2,1)S(1)} %copy-done.14, bf16[4096,1024]{1,0:T(8,128)(2,1)} %all-gather.14.cloned.1.call-done), kind=kOutput, calls=%fused_computation.51 | convolution fusion | flops 1108344832 | bytes 8392704 | tf_op jit(solution)/shard_map/dot_general | solution.py:28
  277.8 75.9 %all-gather.16.cloned.1.call-done = bf16[4096,1024]{0,1:T(8,128)(2,1)} async-done(((bf16[128,1024]{0,1:T(8,128)(2,1)}), bf16[4096,1024]{0,1:T(8,128)(2,1)}) %all-gather.16.cloned.1.call-update) | async-done | bytes 8388624 | tf_op jit(solution)/shard_map/all_gather | solution.py:262
  360.4 12.7 %multiply_convert_fusion.3 = (bf16[512,1024]{1,0:T(8,128)(2,1)S(1)}, f32[512,1024]{1,0:T(8,128)S(1)}, f32[512,1024]{1,0:T(8,128)}) fusion(f32[1024]{0:T(1024)S(1)} %add.195, bf16[512,1024]{1,0:T(8,128)(2,1)S(1)} %copy-done.15, bf16[4096,1024]{1,0:T(8,128)(2,1)S(1)} %copy-done.17), kind=kOutput, calls=%fused_computation.64 | convolution fusion | flops 1108344832 | bytes 8392704 | tf_op jit(solution)/shard_map/dot_general | solution.py:28
  375.3 7.2 multiply_convert_fusion.4
  431.4 14.9 %copy.94 = bf16[8,4,128,1024]{2,1,0,3:T(4,128)(2,1)} copy(bf16[8,4,128,1024]{3,2,0,1:T(8,128)(2,1)} %pad_maximum_fusion.1) | data formatting | bytes 16777216 | tf_op jit(solution)/shard_map/stack | solution.py:269
  446.2 14.6 %reshape.260 = bf16[4096,1024]{0,1:T(8,128)(2,1)} reshape(bf16[8,4,128,1024]{2,1,0,3:T(4,128)(2,1)} %copy.94) | data formatting | bytes 16777216 | tf_op jit(solution)/shard_map/reshape | solution.py:271
  471.9 9.8 %copy.93 = bf16[8,4,128,1024]{3,2,1,0:T(8,128)(2,1)} copy(bf16[8,4,128,1024]{3,2,0,1:T(8,128)(2,1)} %pad_maximum_fusion) | data formatting | bytes 16777216 | tf_op jit(solution)/shard_map/stack | solution.py:269
  485.6 29.1 %all_to_all.10 = bf16[4,512,256]{2,1,0:T(8,128)(2,1)S(1)} all-to-all(bf16[4,512,256]{2,1,0:T(8,128)(2,1)S(1)} %pad_maximum_fusion.3), channel_id=1, replica_groups=mesh['dp'=8,'tensor'=4] {'tensor'}, dimensions={0} | all-to-all | bytes 2097152 | tf_op jit(solution)/shard_map/all_to_all | solution.py:279
  514.8 52.6 %attend_backward.1 = (bf16[2048,256]{1,0:T(8,128)(2,1)S(1)}, bf16[2048,256]{1,0:T(8,128)(2,1)S(1)}, bf16[2048,256]{1,0:T(8,128)(2,1)S(1)}) custom-call(s32[1]{0:T(128)} %copy.113.length_ref, bf16[2048,768]{1,0:T(8,128)(2,1)} %fusion.q_ref.k_ref.v_ref, bf16[2048,768]{1,0:T(8,128)(2,1)} %fusion.q_ref.k_ref.v_ref, bf16[2048,768]{1,0:T(8,128)(2,1)} %fusion.q_ref.k_ref.v_ref, ...), custom_call_target="tpu_custom_call" | custom-call | flops 42949672960 | bytes 10485760 | tf_op jit(solution)/shard_map/attend_backward/pallas_call | solution.py:230
  569.7 7.0 fusion.61
  589.6 20.3 %reduce-scatter.19.cloned.1.call-done = bf16[512,1024]{1,0:T(8,128)(2,1)} async-done(((bf16[4096,1024]{1,0:T(8,128)(2,1)}), bf16[512,1024]{1,0:T(8,128)(2,1)}) %reduce-scatter.19.cloned.1.call-update) | async-done | bytes 1048592 | tf_op jit(solution)/shard_map/reduce_scatter | solution.py:270
  610.7 39.7 %all-reduce.1 = f32[32,320]{1,0:T(8,128)S(1)} all-reduce(f32[32,320]{1,0:T(8,128)S(1)} %pad_maximum_fusion.5), channel_id=8, replica_groups=mesh['dp'=8,'tensor'=4] {'dp','tensor'}, use_global_device_ids=true, to_apply=%region_24.0.clone | all-reduce | flops 10240 | bytes 81920
  654.9 12.9 %all-reduce = f32[8,64]{1,0:T(8,128)S(1)} all-reduce(f32[8,64]{1,0:T(8,128)S(1)} %maximum_bitcast_fusion.1), channel_id=5, replica_groups=mesh['dp'=8,'tensor'=4] {'dp'}, use_global_device_ids=true, to_apply=%region_11.0.clone | all-reduce | flops 512 | bytes 4096
  676.3 75.8 %reduce-scatter.15.cloned.1.call-done = bf16[512,1024]{1,0:T(8,128)(2,1)} async-done(((bf16[2048,1024]{1,0:T(8,128)(2,1)}), bf16[512,1024]{1,0:T(8,128)(2,1)}) %reduce-scatter.15.cloned.1.call-update) | async-done | bytes 1048592 | tf_op jit(solution)/shard_map/reduce_scatter | solution.py:423
  754.9 27.1 %reduce-scatter.29.cloned.1.call-done = bf16[128,1024]{1,0:T(8,128)(2,1)} async-done(((bf16[512,1024]{1,0:T(8,128)(2,1)}), bf16[128,1024]{1,0:T(8,128)(2,1)}) %reduce-scatter.29.cloned.1.call-update) | async-done | bytes 262160
  783.9 26.1 %reduce-scatter.21.cloned.1.call-done = bf16[128,1024]{1,0:T(8,128)(2,1)} async-done(((bf16[512,1024]{1,0:T(8,128)(2,1)}), bf16[128,1024]{1,0:T(8,128)(2,1)}) %reduce-scatter.21.cloned.1.call-update) | async-done | bytes 262160 | tf_op jit(solution)/shard_map/reduce_scatter | solution.py:273
  (285 shorter events, 126.5 us)
Async XLA Ops:
  7.2 5.4 copy-start.27
  7.2 5.4 copy-start.26
  7.3 78.4 %all-gather.8.cloned.1.call-start = ((), (), s32[]{:S(2)}) async-start(), calls=%async_computation.10 | async-start | bytes 1769472 | tf_op jit(solution)/shard_map/all_gather | solution.py:337
  9.0 112.5 %all-gather.10.cloned.1.call-start = ((), (), s32[]{:S(2)}) async-start(), calls=%async_computation.11 | async-start | bytes 5242880 | tf_op jit(solution)/shard_map/all_gather | solution.py:338
  9.7 173.1 %all-gather.12.cloned.1.call-start = ((), (), s32[]{:S(2)}) async-start(), calls=%async_computation.12 | async-start | bytes 2162688 | tf_op jit(solution)/shard_map/all_gather | solution.py:262
  10.4 250.1 %all-gather.14.cloned.1.call-start = ((), (), s32[]{:S(2)}) async-start(), calls=%async_computation.13 | async-start | bytes 8650752 | tf_op jit(solution)/shard_map/all_gather | solution.py:262
  11.0 342.7 %all-gather.16.cloned.1.call-start = ((), (), s32[]{:S(2)}) async-start(), calls=%async_computation.14 | async-start | bytes 8650752 | tf_op jit(solution)/shard_map/all_gather | solution.py:262
  163.4 32.2 %all-to-all-start = ((bf16[4,512,256]{2,1,0:T(8,128)(2,1)}), bf16[4,512,256]{2,1,0:T(8,128)(2,1)S(1)}, u32[]{:S(2)}, u32[]{:S(2)}) async-start(bf16[4,512,256]{2,1,0:T(8,128)(2,1)} %bitcast.5), calls=%async_computation | async-start | bytes 2097152 | tf_op jit(solution)/shard_map/all_to_all | solution.py:279
  166.9 400.7 %reduce-scatter.17.cloned.1.call-start = ((), (), s32[]{:S(2)}) async-start(), calls=%async_computation.16 | async-start | bytes 2359296 | tf_op jit(solution)/shard_map/reduce_scatter | solution.py:270
  182.8 14.3 %copy-start.6 = (bf16[4096,256]{0,1:T(8,128)(2,1)S(1)}, bf16[4096,256]{0,1:T(8,128)(2,1)}, u32[]{:S(2)}) copy-start(bf16[4096,256]{0,1:T(8,128)(2,1)} %all-gather.12.cloned.1.call-done) | copy-start | bytes 6291460
  260.5 8.9 %copy-start.14 = (bf16[512,1024]{1,0:T(8,128)(2,1)S(1)}, bf16[512,1024]{1,0:T(8,128)(2,1)}, u32[]{:S(2)}) copy-start(bf16[512,1024]{1,0:T(8,128)(2,1)} %fusion.28) | copy-start | bytes 3145732
  353.7 6.6 copy-start.17
  357.0 17.1 %slice-start = ((s8[8388608]{0:T(1024)(128)(4,1)}), s8[4194304]{0:T(1024)(128)(4,1)S(1)}, s32[]{:S(2)}) async-start(s8[8388608]{0:T(1024)(128)(4,1)} %bitcast.181), calls=%async_computation.23 | async-start | bytes 8388608
  360.4 13.7 %slice-start.1 = ((s8[8388608]{0:T(1024)(128)(4,1)}), s8[4194304]{0:T(1024)(128)(4,1)S(1)}, s32[]{:S(2)}) async-start(s8[8388608]{0:T(1024)(128)(4,1)} %bitcast.181), calls=%async_computation.24 | async-start | bytes 8388608
  389.8 13.7 %copy-start.10 = (bf16[512,1024]{1,0:T(8,128)(2,1)}, bf16[512,1024]{1,0:T(8,128)(2,1)S(1)}, u32[]{:S(2)}) copy-start(bf16[512,1024]{1,0:T(8,128)(2,1)S(1)} %convert_element_type.172) | copy-start | bytes 3145732
  420.7 165.3 %reduce-scatter.23.cloned.1.call-start = ((), (), s32[]{:S(2)}) async-start(), calls=%async_computation.19 | async-start | bytes 9437184 | tf_op jit(solution)/shard_map/reduce_scatter | solution.py:270
  460.9 149.1 %reduce-scatter.19.cloned.1.call-start = ((), (), s32[]{:S(2)}) async-start(), calls=%async_computation.17 | async-start | bytes 9437184 | tf_op jit(solution)/shard_map/reduce_scatter | solution.py:270
  481.7 188.1 %reduce-scatter.27.cloned.1.call-start = ((), (), s32[]{:S(2)}) async-start(), calls=%async_computation.21 | async-start | bytes 327680
  567.6 11.8 %copy-start.3 = (bf16[2048,768]{1,0:T(8,128)(2,1)}, bf16[2048,768]{1,0:T(8,128)(2,1)S(1)}, u32[]{:S(2)}) copy-start(bf16[2048,768]{1,0:T(8,128)(2,1)S(1)} %constant_dynamic-update-slice_fusion) | copy-start | bytes 9437188
  569.7 103.2 %reduce-scatter.25.cloned.1.call-start = ((), (), s32[]{:S(2)}) async-start(), calls=%async_computation.20 | async-start | bytes 1769472
  579.4 172.7 %reduce-scatter.15.cloned.1.call-start = ((), (), s32[]{:S(2)}) async-start(), calls=%async_computation.15 | async-start | bytes 5242880 | tf_op jit(solution)/shard_map/reduce_scatter | solution.py:423
  585.9 196.1 %reduce-scatter.29.cloned.1.call-start = ((), (), s32[]{:S(2)}) async-start(), calls=%async_computation.22 | async-start | bytes 1310720
  588.3 221.8 %reduce-scatter.21.cloned.1.call-start = ((), (), s32[]{:S(2)}) async-start(), calls=%async_computation.18 | async-start | bytes 1310720 | tf_op jit(solution)/shard_map/reduce_scatter | solution.py:273
  651.8 100.2 %copy-start.2 = (f32[512,1024]{1,0:T(8,128)S(1)}, f32[512,1024]{1,0:T(8,128)}, u32[]{:S(2)}) copy-start(f32[512,1024]{1,0:T(8,128)} %copy-done.1) | copy-start | bytes 6291460
  (42 other events, 104.4 us)
Sparse Core Ops, SparseCore 0:
  10.5 28.3 all-gather.7
  40.5 80.9 all-gather.9
  124.3 58.4 all-gather.11
  185.5 74.9 all-gather.13
  263.2 90.4 all-gather.15
  420.8 39.2 reduce-scatter.16
  463.6 71.2 reduce-scatter.22
  538.4 71.5 reduce-scatter.18
  612.8 19.9 reduce-scatter.26
  635.9 36.8 reduce-scatter.24
  675.2 76.8 reduce-scatter.14
  754.2 27.7 reduce-scatter.28
  784.3 25.7 reduce-scatter.20
